TPU v7x, 256 devices: a whole 4x4x8 slice. The times are simulated.
256 devices in a mesh: ch: 256 (over z, x, y, core).
Axes of the slice: x: 4, y: 4, z: 8, core: 2. Of those that a mesh axis runs over, the one named last changes fastest.
Arguments:
- spectra: bfloat16 [4, 131072, 128], P(None, 'ch'), may hold values from -6 to 6
- offsets: int32 [131072], P('ch'), may hold values from 0 to 7
- bins: int32 [4], replicated, may hold values from 1 to 63
Outputs:
- gradient: float32 [4, 131072, 128], P(None, 'ch')
All inputs are finite; a program needn't handle non-finite values.
Results may differ from a plain program's by a relative error of at most 0.0015.
Values may be sent and summed in bfloat16 or wider, within the bound.
A program may use at most 64 MiB of HBM per device.

v0:
```python
import math

import jax
import jax.numpy as jnp
from jax import lax
from jax.sharding import PartitionSpec as P

spacing_metres = 8
period_metres = 4096
model_amp = 0.5


def shifted(value, axis, steps):
    count = lax.axis_size(axis)
    leading, last = (max(0, -steps), min(count, count - steps))
    return lax.ppermute(value, axis, [(source, source + steps) for source in range(leading, last)])


def block_terms(mine, mine_off, other, other_off, gap, bins):
    windows = mine.shape[2] // 2
    channels = mine.shape[1]
    other_swap = jnp.concatenate([-other[..., windows:], other[..., :windows]], axis=-1)
    mine_swap = jnp.concatenate([mine[..., windows:], -mine[..., :windows]], axis=-1)
    real_part = (
        jnp.einsum("fik,fjk->fij", mine, other, preferred_element_type=jnp.float32) / windows
    )
    imag_part = (
        jnp.einsum("fik,fjk->fij", mine, other_swap, preferred_element_type=jnp.float32) / windows
    )
    rows = jnp.arange(channels, dtype=jnp.int32)
    distance = (
        (gap + rows[None, :] - rows[:, None]) * spacing_metres
        + other_off[None, :]
        - mine_off[:, None]
    )
    wrapped = jnp.mod(bins[:, None, None] * distance[None, :, :], period_metres)
    phase = wrapped.astype(jnp.float32) * (2.0 * math.pi / period_metres)
    grad_real = jnp.tanh(real_part - model_amp * jnp.cos(phase)).astype(jnp.bfloat16)
    grad_imag = jnp.tanh(imag_part - model_amp * jnp.sin(phase)).astype(jnp.bfloat16)
    forward_term = jnp.einsum("fij,fjk->fik", grad_real, other, preferred_element_type=jnp.float32)
    forward_term = forward_term + jnp.einsum(
        "fij,fjk->fik", grad_imag, other_swap, preferred_element_type=jnp.float32
    )
    back_term = jnp.einsum("fij,fik->fjk", grad_real, mine, preferred_element_type=jnp.float32)
    back_term = back_term + jnp.einsum(
        "fij,fik->fjk", grad_imag, mine_swap, preferred_element_type=jnp.float32
    )
    return (forward_term, back_term)


def local(spectra, offsets, bins):
    channels = spectra.shape[1]
    windows = spectra.shape[2] // 2
    off_wire = offsets.astype(jnp.bfloat16)
    partners = [(spectra, off_wire)]
    for distance in range(1, 4):
        partners.append(shifted((spectra, off_wire), "ch", -distance))
    total = jnp.zeros(spectra.shape, jnp.float32)
    returns = []
    for distance in range(4):
        other, other_off = partners[distance]
        forward_term, back_term = block_terms(
            spectra, offsets, other, other_off.astype(jnp.int32), distance * channels, bins
        )
        total = total + forward_term
        returns.append(back_term)
    total = total + returns[0]
    for distance in range(1, 4):
        total = total + shifted(returns[distance].astype(jnp.bfloat16), "ch", distance).astype(
            jnp.float32
        )
    return total / windows


def solution(mesh):
    return jax.shard_map(
        local,
        mesh=mesh,
        in_specs=(P(None, "ch", None), P("ch"), P()),
        out_specs=P(None, "ch", None),
        check_vma=False,
    )
```

profile of v0, /device:TPU:160, one launch (start us, length us, event | category | flops | bytes accessed | tf_op | source)
XLA Modules:
  0.0 217.1 jit_solution(14411797186045009455)
XLA Ops:
  0.0 0.8 fusion.44
  0.8 7.5 %collective-permute-start.3 = (bf16[512]{0:T(512)(128)(2,1)S(1)}, bf16[512]{0:T(512)(128)(2,1)S(1)}, u32[]{:S(2)}, u32[]{:S(2)}) collective-permute-start(bf16[512]{0:T(512)(128)(2,1)S(1)} %get-tuple-element.6), channel_id=1, source_target_pairs={{2,0},{3,1},{4,2},{5,3},{6,4},{7,5},{8,6},{9,7},{10,8},{11,9},{12,... | collective-permute-start | bytes 3080 | tf_op jit(solution)/shard_map/ppermute | solution.py:16
  8.3 1.9 collective-permute-start.1
  10.2 2.6 %collective-permute-start.5 = (bf16[512]{0:T(512)(128)(2,1)S(1)}, bf16[512]{0:T(512)(128)(2,1)S(1)}, u32[]{:S(2)}, u32[]{:S(2)}) collective-permute-start(bf16[512]{0:T(512)(128)(2,1)S(1)} %get-tuple-element.6), channel_id=1, source_target_pairs={{3,0},{4,1},{5,2},{6,3},{7,4},{8,5},{9,6},{10,7},{11,8},{12,9},{13... | collective-permute-start | bytes 3080 | tf_op jit(solution)/shard_map/ppermute | solution.py:16
  12.9 4.4 %collective-permute-start.4 = (bf16[4,512,128]{2,1,0:T(8,128)(2,1)}, bf16[4,512,128]{2,1,0:T(8,128)(2,1)}, u32[]{:S(2)}, u32[]{:S(2)}) collective-permute-start(bf16[4,512,128]{2,1,0:T(8,128)(2,1)} %param.3), channel_id=1, source_target_pairs={{3,0},{4,1},{5,2},{6,3},{7,4},{8,5},{9,6},{10,7},{11,8},{12,9},{13... | collective-permute-start | bytes 1572872 | tf_op jit(solution)/shard_map/ppermute | solution.py:16
  17.3 2.9 %collective-permute-start = (bf16[4,512,128]{2,1,0:T(8,128)(2,1)}, bf16[4,512,128]{2,1,0:T(8,128)(2,1)}, u32[]{:S(2)}, u32[]{:S(2)}) collective-permute-start(bf16[4,512,128]{2,1,0:T(8,128)(2,1)} %param.3), channel_id=1, source_target_pairs={{1,0},{2,1},{3,2},{4,3},{5,4},{6,5},{7,6},{8,7},{9,8},{10,9},{11,1... | collective-permute-start | bytes 1572872 | tf_op jit(solution)/shard_map/ppermute | solution.py:16
  20.2 0.0 copy-start.10
  20.2 2.5 %fusion.45 = (bf16[4,512,64]{2,1,0:T(8,128)(2,1)S(1)}, bf16[4,512,64]{2,1,0:T(8,128)(2,1)}, bf16[4,512,64]{2,1,0:T(8,128)(2,1)S(1)}, bf16[4,512,64]{2,1,0:T(8,128)(2,1)}) fusion(bf16[4,512,128]{2,1,0:T(8,128)(2,1)} %param.3), kind=kLoop, calls=%fused_computation.98 | loop fusion | flops 262144 | bytes 1572864 | tf_op jit(solution)/shard_map/slice | solution.py:22
  22.7 0.3 pad_maximum_fusion.4
  23.0 0.0 collective-permute-done.3
  23.0 2.4 %collective-permute-start.2 = (bf16[4,512,128]{2,1,0:T(8,128)(2,1)S(1)}, bf16[4,512,128]{2,1,0:T(8,128)(2,1)}, u32[]{:S(2)}, u32[]{:S(2)}) collective-permute-start(bf16[4,512,128]{2,1,0:T(8,128)(2,1)S(1)} %copy-done), channel_id=1, source_target_pairs={{2,0},{3,1},{4,2},{5,3},{6,4},{7,5},{8,6},{9,7},{10,8},{11,9},{12,... | collective-permute-start | bytes 1572872 | tf_op jit(solution)/shard_map/ppermute | solution.py:16
  25.5 1.7 add_subtract_fusion.1
  27.2 31.8 %fusion.20 = (f32[4,512,512]{1,2,0:T(8,128)}, f32[4,512,512]{1,2,0:T(8,128)}) fusion(s32[512,512]{0,1:T(8,128)S(1)} %get-tuple-element.19, s32[4]{0:T(128)S(1)} %copy-done.10, s32[512,512]{0,1:T(8,128)S(1)} %get-tuple-element.20), kind=kLoop, calls=%fused_computation.48 | loop fusion | flops 29360128 | bytes 10485776 | tf_op jit(solution)/shard_map/sin | solution.py:39
  59.0 5.3 %copy.5 = f32[4,512,512]{2,1,0:T(8,128)} copy(f32[4,512,512]{1,2,0:T(8,128)} %get-tuple-element.22) | data formatting | bytes 8388608 | tf_op jit(solution)/shard_map/cos | solution.py:38
  64.3 3.0 %tanh_convert_fusion.3 = bf16[4,512,512]{2,1,0:T(8,128)(2,1)S(1)} fusion(f32[4,512,512]{2,1,0:T(8,128)} %copy.5, bf16[4,512,128]{2,1,0:T(8,128)(2,1)S(1)} %copy-done), kind=kOutput, calls=%fused_computation.47 | convolution fusion | flops 272629760 | bytes 6815744 | tf_op jit(solution)/shard_map/fik,fjk->fij/dot_general | solution.py:25
  67.3 5.3 %copy.25 = f32[4,512,512]{2,1,0:T(8,128)} copy(f32[4,512,512]{1,2,0:T(8,128)} %get-tuple-element.21) | data formatting | bytes 8388608 | tf_op jit(solution)/shard_map/sin | solution.py:39
  72.6 0.7 fusion.46
  73.3 18.4 %fusion.19 = bf16[4,512,512]{1,2,0:T(8,128)(2,1)S(1)} fusion(bf16[4,512,128]{2,1,0:T(8,128)(2,1)S(1)} %copy-done, s32[512,512]{0,1:T(8,128)} %copy-done.4, s32[4]{0:T(128)S(1)} %copy-done.10, bf16[4,512,64]{2,1,0:T(8,128)(2,1)} %get-tuple-element.16, bf16[4,512,64]{2,1,0:T(8,128)(2,1)} %get-tuple-element.14), kind=kOutput, calls=%fused_computation.43 | convolution fusion | flops 288358400 | bytes 4194320 | tf_op jit(solution)/shard_map/fik,fjk->fij/dot_general | solution.py:28
  91.8 1.1 convolution_add_fusion.7
  92.9 0.9 fusion.47
  93.8 0.7 convolution_add_fusion.3
  94.5 1.8 slice_negate_fusion
  96.3 1.1 fusion.13
  97.4 0.1 copy-done.3
  97.5 17.5 %tanh_convert_fusion = bf16[4,512,512]{1,2,0:T(8,128)(2,1)S(1)} fusion(bf16[4,512,128]{2,1,0:T(8,128)(2,1)S(1)} %copy-done, bf16[4,512,128]{2,1,0:T(8,128)(2,1)} %collective-permute-done.4, s32[512,512]{0,1:T(8,128)S(1)} %copy-done.3, s32[4]{0:T(128)S(1)} %copy-done.10), kind=kOutput, calls=%fused_computation.44 | convolution fusion | flops 287309824 | bytes 4194320 | tf_op jit(solution)/shard_map/fik,fjk->fij/dot_general | solution.py:25
  115.1 0.7 fusion.50
  115.8 0.9 fusion.32
  116.7 2.3 %collective-permute-start.8 = (bf16[4,512,128]{2,1,0:T(8,128)(2,1)S(1)}, bf16[4,512,128]{2,1,0:T(8,128)(2,1)S(1)}, u32[]{:S(2)}, u32[]{:S(2)}) collective-permute-start(bf16[4,512,128]{2,1,0:T(8,128)(2,1)S(1)} %fusion.32), channel_id=1, source_target_pairs={{0,3},{1,4},{2,5},{3,6},{4,7},{5,8},{6,9},{7,10},{8,11},{9,12},{10... | collective-permute-start | bytes 1572872 | tf_op jit(solution)/shard_map/ppermute | solution.py:16
  119.0 1.4 slice_negate_fusion.2
  120.5 17.2 %fusion.17 = bf16[4,512,512]{1,2,0:T(8,128)(2,1)S(1)} fusion(bf16[4,512,128]{2,1,0:T(8,128)(2,1)S(1)} %copy-done, s32[512,512]{0,1:T(8,128)S(1)} %copy-done.7, s32[4]{0:T(128)S(1)} %copy-done.10, bf16[4,512,64]{2,1,0:T(8,128)(2,1)S(1)} %get-tuple-element.10, bf16[4,512,64]{2,1,0:T(8,128)(2,1)S(1)} %get-tuple-element.9), kind=kOutput, calls=%fused_computation.40 | convolution fusion | flops 288358400 | bytes 4194320 | tf_op jit(solution)/shard_map/fik,fjk->fij/dot_general | solution.py:28
  137.7 0.0 copy-start.8
  137.7 0.8 fusion.33
  138.5 1.0 fusion.35
  139.5 17.6 %tanh_convert_fusion.1 = bf16[4,512,512]{1,2,0:T(8,128)(2,1)S(1)} fusion(bf16[4,512,128]{2,1,0:T(8,128)(2,1)S(1)} %copy-done, bf16[4,512,128]{2,1,0:T(8,128)(2,1)} %collective-permute-done.2, s32[512,512]{0,1:T(8,128)S(1)} %copy-done.8, s32[4]{0:T(128)S(1)} %copy-done.10), kind=kOutput, calls=%fused_computation.45 | convolution fusion | flops 287309824 | bytes 4194320 | tf_op jit(solution)/shard_map/fik,fjk->fij/dot_general | solution.py:25
  157.1 0.7 fusion.49
  157.8 1.4 slice_negate_fusion.1
  159.3 17.0 %fusion.15 = bf16[4,512,512]{1,2,0:T(8,128)(2,1)S(1)} fusion(bf16[4,512,128]{2,1,0:T(8,128)(2,1)S(1)} %copy-done, s32[512,512]{0,1:T(8,128)S(1)} %copy-done.8, s32[4]{0:T(128)S(1)} %copy-done.10, bf16[4,512,64]{2,1,0:T(8,128)(2,1)S(1)} %get-tuple-element.8, bf16[4,512,64]{2,1,0:T(8,128)(2,1)S(1)} %get-tuple-element.7), kind=kOutput, calls=%fused_computation.37 | convolution fusion | flops 288358400 | bytes 4194320 | tf_op jit(solution)/shard_map/fik,fjk->fij/dot_general | solution.py:28
  176.2 0.7 fusion.31
  176.9 3.0 %collective-permute-start.7 = (bf16[4,512,128]{2,1,0:T(8,128)(2,1)S(1)}, bf16[4,512,128]{2,1,0:T(8,128)(2,1)S(1)}, u32[]{:S(2)}, u32[]{:S(2)}) collective-permute-start(bf16[4,512,128]{2,1,0:T(8,128)(2,1)S(1)} %fusion.31), channel_id=1, source_target_pairs={{0,2},{1,3},{2,4},{3,5},{4,6},{5,7},{6,8},{7,9},{8,10},{9,11},{10,... | collective-permute-start | bytes 1572872 | tf_op jit(solution)/shard_map/ppermute | solution.py:16
  180.0 17.8 %tanh_convert_fusion.2 = bf16[4,512,512]{1,2,0:T(8,128)(2,1)S(1)} fusion(bf16[4,512,128]{2,1,0:T(8,128)(2,1)S(1)} %copy-done, bf16[4,512,128]{2,1,0:T(8,128)(2,1)} %collective-permute-done, s32[512,512]{0,1:T(8,128)S(1)} %copy-done.7, s32[4]{0:T(128)S(1)} %copy-done.10), kind=kOutput, calls=%fused_computation.46 | convolution fusion | flops 287309824 | bytes 4194320 | tf_op jit(solution)/shard_map/fik,fjk->fij/dot_general | solution.py:25
  197.8 0.7 fusion.48
  198.5 0.7 fusion.30
  199.2 1.9 collective-permute-start.6
  201.2 1.9 convolution_add_fusion.4
  203.1 1.0 fusion.34
  204.1 1.9 fusion.29
  206.1 7.9 %collective-permute-done.6 = bf16[4,512,128]{2,1,0:T(8,128)(2,1)S(1)} collective-permute-done((bf16[4,512,128]{2,1,0:T(8,128)(2,1)S(1)}, bf16[4,512,128]{2,1,0:T(8,128)(2,1)S(1)}, u32[]{:S(2)}, u32[]{:S(2)}) %collective-permute-start.6) | collective-permute-done | bytes 524320 | tf_op jit(solution)/shard_map/ppermute | solution.py:16
  214.0 3.1 %fusion.28 = f32[4,512,128]{2,1,0:T(8,128)} fusion(f32[4,512,128]{2,1,0:T(8,128)S(1)} %convolution_add_fusion.3, f32[4,512,128]{2,1,0:T(8,128)S(1)} %convolution_add_fusion.4, f32[4,512,128]{2,1,0:T(8,128)S(1)} %fusion.29, f32[4,512,128]{2,1,0:T(8,128)S(1)} %fusion.34, bf16[4,512,512]{1,2,0:T(8,128)(2,1)S(1)} %tanh_convert_fusion.1, ...), kind=kOutput, calls=%fused_computation.62 | convolution fusion | flops 271319040 | bytes 9437184 | tf_op jit(solution)/shard_map/fij,fjk->fik/dot_general | solution.py:40
  (31 shorter events, 0.1 us)
Async XLA Ops:
  0.0 25.5 %copy-start.9 = (s32[512]{0:T(512)S(1)}, s32[512]{0:T(512)}, u32[]{:S(2)}) copy-start(s32[512]{0:T(512)} %param.4) | copy-start | bytes 6148
  0.0 23.0 %copy-start = (bf16[4,512,128]{2,1,0:T(8,128)(2,1)S(1)}, bf16[4,512,128]{2,1,0:T(8,128)(2,1)}, u32[]{:S(2)}) copy-start(bf16[4,512,128]{2,1,0:T(8,128)(2,1)} %param.3) | copy-start | bytes 1572868
  0.8 22.2 %collective-permute-start.3 = (bf16[512]{0:T(512)(128)(2,1)S(1)}, bf16[512]{0:T(512)(128)(2,1)S(1)}, u32[]{:S(2)}, u32[]{:S(2)}) collective-permute-start(bf16[512]{0:T(512)(128)(2,1)S(1)} %get-tuple-element.6), channel_id=1, source_target_pairs={{2,0},{3,1},{4,2},{5,3},{6,4},{7,5},{8,6},{9,7},{10,8},{11,9},{12,... | collective-permute-start | bytes 3080 | tf_op jit(solution)/shard_map/ppermute | solution.py:16
  8.3 17.1 %collective-permute-start.1 = (bf16[512]{0:T(512)(128)(2,1)S(1)}, bf16[512]{0:T(512)(128)(2,1)S(1)}, u32[]{:S(2)}, u32[]{:S(2)}) collective-permute-start(bf16[512]{0:T(512)(128)(2,1)S(1)} %get-tuple-element.6), channel_id=1, source_target_pairs={{1,0},{2,1},{3,2},{4,3},{5,4},{6,5},{7,6},{8,7},{9,8},{10,9},{11,1... | collective-permute-start | bytes 3080 | tf_op jit(solution)/shard_map/ppermute | solution.py:16
  10.2 15.2 %collective-permute-start.5 = (bf16[512]{0:T(512)(128)(2,1)S(1)}, bf16[512]{0:T(512)(128)(2,1)S(1)}, u32[]{:S(2)}, u32[]{:S(2)}) collective-permute-start(bf16[512]{0:T(512)(128)(2,1)S(1)} %get-tuple-element.6), channel_id=1, source_target_pairs={{3,0},{4,1},{5,2},{6,3},{7,4},{8,5},{9,6},{10,7},{11,8},{12,9},{13... | collective-permute-start | bytes 3080 | tf_op jit(solution)/shard_map/ppermute | solution.py:16
  12.9 81.6 %collective-permute-start.4 = (bf16[4,512,128]{2,1,0:T(8,128)(2,1)}, bf16[4,512,128]{2,1,0:T(8,128)(2,1)}, u32[]{:S(2)}, u32[]{:S(2)}) collective-permute-start(bf16[4,512,128]{2,1,0:T(8,128)(2,1)} %param.3), channel_id=1, source_target_pairs={{3,0},{4,1},{5,2},{6,3},{7,4},{8,5},{9,6},{10,7},{11,8},{12,9},{13... | collective-permute-start | bytes 1572872 | tf_op jit(solution)/shard_map/ppermute | solution.py:16
  17.3 101.7 %collective-permute-start = (bf16[4,512,128]{2,1,0:T(8,128)(2,1)}, bf16[4,512,128]{2,1,0:T(8,128)(2,1)}, u32[]{:S(2)}, u32[]{:S(2)}) collective-permute-start(bf16[4,512,128]{2,1,0:T(8,128)(2,1)} %param.3), channel_id=1, source_target_pairs={{1,0},{2,1},{3,2},{4,3},{5,4},{6,5},{7,6},{8,7},{9,8},{10,9},{11,1... | collective-permute-start | bytes 1572872 | tf_op jit(solution)/shard_map/ppermute | solution.py:16
  20.2 7.0 %copy-start.10 = (s32[4]{0:T(128)S(1)}, s32[4]{0:T(128)}, u32[]{:S(2)}) copy-start(s32[4]{0:T(128)} %param.5) | copy-start | bytes 52
  23.0 116.5 %collective-permute-start.2 = (bf16[4,512,128]{2,1,0:T(8,128)(2,1)S(1)}, bf16[4,512,128]{2,1,0:T(8,128)(2,1)}, u32[]{:S(2)}, u32[]{:S(2)}) collective-permute-start(bf16[4,512,128]{2,1,0:T(8,128)(2,1)S(1)} %copy-done), channel_id=1, source_target_pairs={{2,0},{3,1},{4,2},{5,3},{6,4},{7,5},{8,6},{9,7},{10,8},{11,9},{12,... | collective-permute-start | bytes 1572872 | tf_op jit(solution)/shard_map/ppermute | solution.py:16
  27.2 31.8 %copy-start.2 = (s32[512,512]{0,1:T(8,128)}, s32[512,512]{0,1:T(8,128)S(1)}, u32[]{:S(2)}) copy-start(s32[512,512]{0,1:T(8,128)S(1)} %get-tuple-element.19) | copy-start | bytes 3145732
  27.2 31.8 %copy-start.4 = (s32[512,512]{0,1:T(8,128)}, s32[512,512]{0,1:T(8,128)S(1)}, u32[]{:S(2)}) copy-start(s32[512,512]{0,1:T(8,128)S(1)} %get-tuple-element.20) | copy-start | bytes 3145732
  73.3 18.4 %copy-start.5 = (bf16[4,512,64]{2,1,0:T(8,128)(2,1)S(1)}, bf16[4,512,64]{2,1,0:T(8,128)(2,1)}, u32[]{:S(2)}) copy-start(bf16[4,512,64]{2,1,0:T(8,128)(2,1)} %get-tuple-element.14) | copy-start | bytes 786436
  73.3 18.4 %copy-start.6 = (bf16[4,512,64]{2,1,0:T(8,128)(2,1)S(1)}, bf16[4,512,64]{2,1,0:T(8,128)(2,1)}, u32[]{:S(2)}) copy-start(bf16[4,512,64]{2,1,0:T(8,128)(2,1)} %get-tuple-element.16) | copy-start | bytes 786436
  93.8 2.6 %copy-start.1 = (f32[4,512,512]{2,1,0:T(8,128)S(1)}, f32[4,512,512]{2,1,0:T(8,128)}, u32[]{:S(2)}) copy-start(f32[4,512,512]{2,1,0:T(8,128)} %copy.25) | copy-start | bytes 12582916
  96.3 1.2 copy-start.3
  115.1 5.4 %copy-start.7 = (s32[512,512]{0,1:T(8,128)S(1)}, s32[512,512]{0,1:T(8,128)}, u32[]{:S(2)}) copy-start(s32[512,512]{0,1:T(8,128)} %get-tuple-element.18) | copy-start | bytes 3145732
  116.7 89.4 %collective-permute-start.8 = (bf16[4,512,128]{2,1,0:T(8,128)(2,1)S(1)}, bf16[4,512,128]{2,1,0:T(8,128)(2,1)S(1)}, u32[]{:S(2)}, u32[]{:S(2)}) collective-permute-start(bf16[4,512,128]{2,1,0:T(8,128)(2,1)S(1)} %fusion.32), channel_id=1, source_target_pairs={{0,3},{1,4},{2,5},{3,6},{4,7},{5,8},{6,9},{7,10},{8,11},{9,12},{10... | collective-permute-start | bytes 1572872 | tf_op jit(solution)/shard_map/ppermute | solution.py:16
  137.7 1.9 copy-start.8
  176.9 29.1 %collective-permute-start.7 = (bf16[4,512,128]{2,1,0:T(8,128)(2,1)S(1)}, bf16[4,512,128]{2,1,0:T(8,128)(2,1)S(1)}, u32[]{:S(2)}, u32[]{:S(2)}) collective-permute-start(bf16[4,512,128]{2,1,0:T(8,128)(2,1)S(1)} %fusion.31), channel_id=1, source_target_pairs={{0,2},{1,3},{2,4},{3,5},{4,6},{5,7},{6,8},{7,9},{8,10},{9,11},{10,... | collective-permute-start | bytes 1572872 | tf_op jit(solution)/shard_map/ppermute | solution.py:16
  199.2 14.7 %collective-permute-start.6 = (bf16[4,512,128]{2,1,0:T(8,128)(2,1)S(1)}, bf16[4,512,128]{2,1,0:T(8,128)(2,1)S(1)}, u32[]{:S(2)}, u32[]{:S(2)}) collective-permute-start(bf16[4,512,128]{2,1,0:T(8,128)(2,1)S(1)} %fusion.30), channel_id=1, source_target_pairs={{0,1},{1,2},{2,3},{3,4},{4,5},{5,6},{6,7},{7,8},{8,9},{9,10},{10,1... | collective-permute-start | bytes 1572872 | tf_op jit(solution)/shard_map/ppermute | solution.py:16
where the time goes:
time: 218 us; the launch traced here: 217 us
  matrix products  127 us (58%)
  other arithmetic  41.7 us (19%)
  starting transfers between devices  29 us (13%)
  local copies, waits for them, and re-layouts  10.8 us (5%)
  waiting for transfers between devices  7.88 us (4%)
    dot_general x4, matrix products, block_terms(): jnp.einsum('fik,fjk->fij', mine, other, preferred_element_type=jnp.float32)  55.9 us
    dot_general x4, matrix products, block_terms(): jnp.einsum('fik,fjk->fij', mine, other_swap, preferred_element_type=jnp.f...  53.6 us
    sin x1, other arithmetic, block_terms(): jnp.sin(phase)  31.8 us
    ppermute x9, starting transfers between devices, shifted(): lax.ppermute(value, axis, [(source, source + steps) for source in range(l...  29 us
    ppermute x9, waiting for transfers between devices, shifted(): lax.ppermute(value, axis, [(source, source + steps) for source in range(l...  7.88 us
    dot_general x4, matrix products, block_terms(): jnp.einsum('fij,fjk->fik', grad_real, other, preferred_element_type=jnp.f...  7.68 us
    sin x1, local copies, waits for them, and re-layouts, block_terms(): jnp.sin(phase)  5.34 us
    cos x1, local copies, waits for them, and re-layouts, block_terms(): jnp.cos(phase)  5.27 us
  transfers between devices with their start and end apart: 9, of which 1 were waited for; matrix products, arithmetic and copies ran while one was open for 81% of the time, Pallas kernels for 0%

commit v1 on v0

v1 whole, which is shorter than its diff:
```python
import functools
import math

import jax
import jax.numpy as jnp
from jax import lax
from jax.experimental import pallas as pl
from jax.experimental.pallas import tpu as pltpu
from jax.sharding import PartitionSpec as P

spacing_metres = 8
period_metres = 4096
model_amp = 0.5

F32 = jnp.float32
BF16 = jnp.bfloat16
MESH = pl.DeviceIdType.MESH

OWN, PARTNER, M_SAME, P_SAME, M_OTHER, P_OTHER, FAR = range(7)
TO_PARTNER, TO_PLUS, TO_MINUS, FWD_M, FWD_P, FWD_FAR = range(6)


def dot(a, b):
    return lax.dot_general(a, b, (((1,), (0,)), ((), ())), preferred_element_type=F32)


def cos_sin(m):
    quarter = period_metres // 4
    turn = (m + quarter // 2) // quarter
    theta = (m - turn * quarter).astype(F32) * (2.0 * math.pi / period_metres)
    x = theta * theta
    s = theta * (1.0 + x * (-1.0 / 6 + x * (1.0 / 120 + x * (-1.0 / 5040 + x * (1.0 / 362880)))))
    c = 1.0 + x * (-0.5 + x * (1.0 / 24 + x * (-1.0 / 720 + x * (1.0 / 40320))))
    turn = turn & 3
    odd = (turn & 1) == 1
    cos = jnp.where(odd, s, c)
    sin = jnp.where(odd, c, s)
    cos = jnp.where((turn == 1) | (turn == 2), -cos, cos)
    sin = jnp.where(turn >= 2, -sin, sin)
    return cos, sin


def split(v):
    high = v.astype(BF16).astype(F32)
    return high, v - high


def kernel(nfreq, nch, ndev, bins_ref, off_ref, spec_ref, out_ref, blk, aug, wre, wim, acc, offs,
           local_sem, send_sem, recv_sem, off_send, off_recv):
    lanes = 128
    groups = nch // lanes
    me = lax.axis_index("ch")
    nchip = ndev // 2
    chip = me // 2
    core = me - 2 * chip
    up = lax.rem(chip + 1, nchip)
    down = lax.rem(chip + nchip - 1, nchip)
    partner = 2 * chip + (1 - core)
    plus_same, plus_other = 2 * up + core, 2 * up + (1 - core)
    minus_same, minus_other = 2 * down + core, 2 * down + (1 - core)
    far_to = jnp.where(core == 1, plus_other, minus_other)
    far_from = jnp.where(core == 1, M_SAME, P_SAME)

    barrier = pltpu.get_barrier_semaphore()
    for peer in (partner, plus_same, minus_same, plus_other, minus_other):
        pl.semaphore_signal(barrier, inc=1, device_id=(peer,), device_id_type=MESH)

    def own_load(f):
        return pltpu.make_async_copy(spec_ref.at[f], blk.at[OWN, f], local_sem.at[f])

    for f in range(nfreq):
        own_load(f).start()

    aug[...] = jnp.zeros_like(aug)
    wre[:, lanes:, :] = jnp.zeros((nfreq, wre.shape[1] - lanes, nch), BF16)
    wim[:, lanes:, :] = jnp.zeros((nfreq, wim.shape[1] - lanes, nch), BF16)

    def send(kind, f, src, slot, to):
        return pltpu.make_async_remote_copy(
            src_ref=src, dst_ref=blk.at[slot, f], send_sem=send_sem.at[kind, f],
            recv_sem=recv_sem.at[slot, f], device_id=(to,), device_id_type=MESH)

    def sends(f):
        return (
            send(TO_PLUS, f, spec_ref.at[f], M_SAME, plus_same),
            send(TO_MINUS, f, spec_ref.at[f], P_SAME, minus_same),
            send(TO_PARTNER, f, spec_ref.at[f], PARTNER, partner),
        )

    def forwards(f):
        return (
            send(FWD_M, f, blk.at[M_SAME, f], M_OTHER, partner),
            send(FWD_P, f, blk.at[P_SAME, f], P_OTHER, partner),
            send(FWD_FAR, f, blk.at[far_from, f], FAR, far_to),
        )

    def off_copy(n, src, slot, to):
        return pltpu.make_async_remote_copy(
            src_ref=src, dst_ref=offs.at[slot], send_sem=off_send.at[n],
            recv_sem=off_recv.at[slot], device_id=(to,), device_id_type=MESH)

    off_sends = (
        off_copy(0, off_ref, PARTNER, partner),
        off_copy(1, off_ref, M_SAME, plus_same),
        off_copy(2, off_ref, P_SAME, minus_same),
        off_copy(3, off_ref, M_OTHER, plus_other),
        off_copy(4, off_ref, P_OTHER, minus_other),
    )
    off_far = off_copy(5, offs.at[far_from], FAR, far_to)

    def wait_block(slot, f):
        send(TO_PLUS, f, spec_ref.at[f], slot, plus_same).wait_recv()

    row = lax.broadcasted_iota(jnp.int32, (8, lanes), 0)
    part = row & 3

    def pick(parts, a, b, c, d):
        return jnp.where(parts == 0, a, jnp.where(parts == 1, b, jnp.where(parts == 2, c, d)))

    def tables(off):
        shape = off.shape
        place = lax.broadcasted_iota(jnp.int32, shape, 1) * lanes + lax.broadcasted_iota(jnp.int32, shape, 2)
        pos = place * spacing_metres + off
        result = []
        for f in range(nfreq):
            cos, sin = cos_sin((bins_ref[f] * pos) & (period_metres - 1))
            result.append(split(cos) + split(sin))
        return result

    def put_aug(slot, table, n):
        for g in range(groups):
            rows = []
            for f in range(nfreq):
                ch, cl, sh, sl = (v[n, g : g + 1, :] for v in table[f])
                rows.append(pick(part, ch, cl, sh, sl))
            block = jnp.concatenate(rows, axis=0)
            aug[slot, g * lanes : (g + 1) * lanes, 0 : 8 * nfreq] = block.T.astype(BF16)

    own_table = tables(off_ref[...].reshape(1, groups, lanes))
    put_aug(OWN, own_table, 0)
    late = row >= 4
    cosine = part < 2
    nothing = jnp.zeros((8, lanes), F32)
    for g in range(groups):
        for f in range(nfreq):
            ch, cl, sh, sl = (v[0, g : g + 1, :] for v in own_table[f])
            cos = jnp.where(late, cl, ch)
            sin = jnp.where(late, sl, sh)
            real = jnp.where(cosine, cos, sin) * (-model_amp)
            imag = jnp.where(cosine, sin, -cos) * model_amp
            cols = slice(g * lanes, (g + 1) * lanes)
            rows = slice(lanes, lanes + 8 * nfreq)
            wre[f, rows, cols] = jnp.concatenate(
                [real if n == f else nothing for n in range(nfreq)], axis=0).astype(BF16)
            wim[f, rows, cols] = jnp.concatenate(
                [imag if n == f else nothing for n in range(nfreq)], axis=0).astype(BF16)

    pl.semaphore_wait(barrier, 5)
    for copy in off_sends:
        copy.start()
    for f in range(nfreq):
        for copy in sends(f):
            copy.start()

    half = lanes // 2
    scale = 1.0 / half

    def transposed(slot, f):
        t = blk[slot, f].T
        return t, jnp.concatenate([-t[half:], t[:half]], axis=0)

    def grads(slot, f):
        x = jnp.concatenate([blk[slot, f], aug[slot]], axis=1)
        real = jnp.tanh(dot(x, wre[f])).astype(BF16)
        imag = jnp.tanh(dot(x, wim[f])).astype(BF16)
        return real, imag

    def terms(slot, f, g):
        t, swapped = transposed(slot, f)
        return dot(t, g[0]) + dot(swapped, g[1])

    def own_step(i, carry):
        fs = [2 * i, 2 * i + 1]
        for f in fs:
            own_load(f).wait()
            t, swapped = transposed(OWN, f)
            wre[f, :lanes, :] = t * jnp.array(scale, BF16)
            wim[f, :lanes, :] = swapped * jnp.array(-scale, BF16)
        g = [grads(OWN, f) for f in fs]
        for f, v in zip(fs, g):
            acc[f] = 2.0 * terms(OWN, f, v)
        return carry

    lax.fori_loop(0, nfreq // 2, own_step, 0)

    for slot in (PARTNER, M_SAME, P_SAME, M_OTHER, P_OTHER):
        off_copy(0, off_ref, slot, partner).wait_recv()
    off_far.start()
    table = tables(offs[PARTNER : P_OTHER + 1])
    for slot in range(PARTNER, P_OTHER + 1):
        put_aug(slot, table, slot - PARTNER)

    def partner_step(i, carry):
        fs = [2 * i, 2 * i + 1]
        for f in fs:
            wait_block(PARTNER, f)
        g = [grads(PARTNER, f) for f in fs]
        for f, v in zip(fs, g):
            acc[f] += terms(PARTNER, f, v)
        return carry

    lax.fori_loop(0, nfreq // 2, partner_step, 0)

    has_m = jnp.where(chip >= 1, 1.0, 0.0).astype(F32)
    has_p = jnp.where(chip < nchip - 1, 1.0, 0.0).astype(F32)
    has_far = jnp.where(core == 1, chip < nchip - 2, chip >= 2)
    has_far = jnp.where(has_far, 1.0, 0.0).astype(F32)

    def pair(m_slot, p_slot, f):
        gm = grads(m_slot, f)
        gp = grads(p_slot, f)
        acc[f] += has_m * terms(m_slot, f, gm) + has_p * terms(p_slot, f, gp)

    def near_step(f, carry):
        wait_block(M_SAME, f)
        wait_block(P_SAME, f)
        for copy in forwards(f):
            copy.start()
        pair(M_SAME, P_SAME, f)
        wait_block(M_OTHER, f)
        wait_block(P_OTHER, f)
        pair(M_OTHER, P_OTHER, f)
        return carry

    lax.fori_loop(0, nfreq, near_step, 0)

    off_copy(0, off_ref, FAR, partner).wait_recv()
    put_aug(FAR, tables(offs[FAR : FAR + 1]), 0)

    def far_step(f, carry):
        wait_block(FAR, f)
        total = acc[f] + has_far * terms(FAR, f, grads(FAR, f))
        out_ref[f] = total.T * scale
        return carry

    lax.fori_loop(0, nfreq, far_step, 0)

    for copy in off_sends + (off_far,):
        copy.wait_send()
    for f in range(nfreq):
        for copy in sends(f) + forwards(f):
            copy.wait_send()


def local(ndev, spectra, offsets, bins):
    nfreq, nch, width = spectra.shape
    lanes = 128
    assert width == lanes and nch % lanes == 0 and nfreq % 2 == 0 and 8 * nfreq <= lanes
    assert (nch * spacing_metres) % period_metres == 0
    vmem = pl.BlockSpec(memory_space=pltpu.VMEM)
    return pl.pallas_call(
        functools.partial(kernel, nfreq, nch, ndev),
        out_shape=jax.ShapeDtypeStruct((nfreq, nch, width), F32),
        in_specs=[pl.BlockSpec(memory_space=pltpu.SMEM), vmem, pl.BlockSpec(memory_space=pl.ANY)],
        out_specs=vmem,
        scratch_shapes=[
            pltpu.VMEM((7, nfreq, nch, width), BF16),
            pltpu.VMEM((7, nch, lanes), BF16),
            pltpu.VMEM((nfreq, 2 * lanes, nch), BF16),
            pltpu.VMEM((nfreq, 2 * lanes, nch), BF16),
            pltpu.VMEM((nfreq, width, nch), F32),
            pltpu.VMEM((7, nch // lanes, lanes), jnp.int32),
            pltpu.SemaphoreType.DMA((nfreq,)),
            pltpu.SemaphoreType.DMA((6, nfreq)),
            pltpu.SemaphoreType.DMA((7, nfreq)),
            pltpu.SemaphoreType.DMA((6,)),
            pltpu.SemaphoreType.DMA((7,)),
        ],
        compiler_params=pltpu.CompilerParams(
            collective_id=0, has_side_effects=True, vmem_limit_bytes=56 << 20),
    )(bins, offsets.reshape(nch // lanes, lanes), spectra)


def solution(mesh):
    return jax.shard_map(
        functools.partial(local, mesh.shape["ch"]),
        mesh=mesh,
        in_specs=(P(None, "ch", None), P("ch"), P()),
        out_specs=P(None, "ch", None),
        check_vma=False,
    )
```

time: 218 us -> 36.9 us (0.17)
  the two profiles are of different devices: /device:TPU:160 before, /device:TPU:0 now
where the time goes in v1:
time: 36.9 us; the launch traced here: 36.7 us
  Pallas kernels  34.5 us (93%)
  local copies, waits for them, and re-layouts  2.26 us (6%)
    pallas_call x1, Pallas kernels, local(): pl.pallas_call(functools.partial(kernel, nfreq, nch, ndev), out_shape=jax...  34.5 us
    unnamed x1, local copies, waits for them, and re-layouts  2.26 us

profile of v1, /device:TPU:0, one launch (start us, length us, event | category | flops | bytes accessed | tf_op | source)
XLA Modules:
  0.0 36.7 jit_solution(15472481834555378882)
XLA Ops:
  0.0 34.5 %shard_map.37 = f32[4,512,128]{2,1,0:T(8,128)} custom-call(s32[4]{0:T(128)} %bins_ref.1, s32[4,128]{1,0:T(4,128)} %bitcast.1, bf16[4,512,128]{2,1,0:T(8,128)(2,1)} %spec_ref.1), custom_call_target="tpu_custom_call" | custom-call | tf_op jit(solution)/shard_map/pallas_call | solution.py:261
  34.5 2.3 %copy.5 = f32[4,512,128]{2,1,0:T(8,128)} copy(f32[4,512,128]{2,1,0:T(8,128)} %shard_map.37) | data formatting | bytes 2097152

commit v2 on v1

--- a/solution.py
+++ b/solution.py
@@ -45,31 +45,71 @@
     return high, v - high
 
 
-def kernel(nfreq, nch, ndev, bins_ref, off_ref, spec_ref, out_ref, blk, aug, wre, wim, acc, offs,
-           local_sem, send_sem, recv_sem, off_send, off_recv):
+def kernel(nfreq, nch, ndev, bins_hbm, off_ref, spec_ref, out_ref, blk, aug, wre, wim, acc, res, offs, bins_ref,
+           in_sem, local_sem, out_sem, send_sem, recv_sem, off_send, off_recv):
     lanes = 128
     groups = nch // lanes
     me = lax.axis_index("ch")
     nchip = ndev // 2
     chip = me // 2
     core = me - 2 * chip
-    up = lax.rem(chip + 1, nchip)
-    down = lax.rem(chip + nchip - 1, nchip)
+    up = jnp.minimum(chip + 1, nchip - 1)
+    down = jnp.maximum(chip - 1, 0)
+    has_up = chip < nchip - 1
+    has_down = chip >= 1
     partner = 2 * chip + (1 - core)
     plus_same, plus_other = 2 * up + core, 2 * up + (1 - core)
     minus_same, minus_other = 2 * down + core, 2 * down + (1 - core)
-    far_to = jnp.where(core == 1, plus_other, minus_other)
-    far_from = jnp.where(core == 1, M_SAME, P_SAME)
+    upward = core == 1
+    far_to = jnp.where(upward, plus_other, minus_other)
+    far_from = jnp.where(upward, M_SAME, P_SAME)
+    sends_far = has_up & has_down
+    has_far = jnp.where(upward, chip < nchip - 2, chip >= 2)
 
     barrier = pltpu.get_barrier_semaphore()
-    for peer in (partner, plus_same, minus_same, plus_other, minus_other):
+
+    def greet(peer):
         pl.semaphore_signal(barrier, inc=1, device_id=(peer,), device_id_type=MESH)
+
+    @pl.when(has_up)
+    def _():
+        greet(plus_same)
+        greet(plus_other)
+
+    @pl.when(has_down)
+    def _():
+        greet(minus_same)
+        greet(minus_other)
+
+    greet(partner)
 
     def own_load(f):
         return pltpu.make_async_copy(spec_ref.at[f], blk.at[OWN, f], local_sem.at[f])
 
+    bins_load = pltpu.make_async_copy(bins_hbm, bins_ref, in_sem.at[0])
+    off_load = pltpu.make_async_copy(off_ref, offs.at[OWN], in_sem.at[1])
+    bins_load.start()
+    off_load.start()
     for f in range(nfreq):
         own_load(f).start()
+
+    def clear(slots, freqs):
+        for slot in slots:
+            offs[slot] = jnp.zeros(offs.shape[1:], offs.dtype)
+            for f in range(freqs):
+                blk[slot, f] = jnp.zeros(blk.shape[2:], blk.dtype)
+
+    @pl.when(jnp.logical_not(has_down))
+    def _():
+        clear((M_SAME, M_OTHER), nfreq)
+
+    @pl.when(jnp.logical_not(has_up))
+    def _():
+        clear((P_SAME, P_OTHER), nfreq)
+
+    @pl.when(jnp.logical_not(has_far))
+    def _():
+        clear((FAR,), nfreq)
 
     aug[...] = jnp.zeros_like(aug)
     wre[:, lanes:, :] = jnp.zeros((nfreq, wre.shape[1] - lanes, nch), BF16)
@@ -80,36 +120,39 @@
             src_ref=src, dst_ref=blk.at[slot, f], send_sem=send_sem.at[kind, f],
             recv_sem=recv_sem.at[slot, f], device_id=(to,), device_id_type=MESH)
 
-    def sends(f):
-        return (
-            send(TO_PLUS, f, spec_ref.at[f], M_SAME, plus_same),
-            send(TO_MINUS, f, spec_ref.at[f], P_SAME, minus_same),
-            send(TO_PARTNER, f, spec_ref.at[f], PARTNER, partner),
-        )
-
-    def forwards(f):
-        return (
-            send(FWD_M, f, blk.at[M_SAME, f], M_OTHER, partner),
-            send(FWD_P, f, blk.at[P_SAME, f], P_OTHER, partner),
-            send(FWD_FAR, f, blk.at[far_from, f], FAR, far_to),
-        )
+    def to_plus(f):
+        return send(TO_PLUS, f, spec_ref.at[f], M_SAME, plus_same)
+
+    def to_minus(f):
+        return send(TO_MINUS, f, spec_ref.at[f], P_SAME, minus_same)
+
+    def to_partner(f):
+        return send(TO_PARTNER, f, spec_ref.at[f], PARTNER, partner)
+
+    def forward_m(f):
+        return send(FWD_M, f, blk.at[M_SAME, f], M_OTHER, partner)
+
+    def forward_p(f):
+        return send(FWD_P, f, blk.at[P_SAME, f], P_OTHER, partner)
+
+    def forward_far(f):
+        return send(FWD_FAR, f, blk.at[far_from, f], FAR, far_to)
 
     def off_copy(n, src, slot, to):
         return pltpu.make_async_remote_copy(
             src_ref=src, dst_ref=offs.at[slot], send_sem=off_send.at[n],
             recv_sem=off_recv.at[slot], device_id=(to,), device_id_type=MESH)
 
-    off_sends = (
-        off_copy(0, off_ref, PARTNER, partner),
-        off_copy(1, off_ref, M_SAME, plus_same),
-        off_copy(2, off_ref, P_SAME, minus_same),
-        off_copy(3, off_ref, M_OTHER, plus_other),
-        off_copy(4, off_ref, P_OTHER, minus_other),
-    )
+    off_partner = off_copy(0, off_ref, PARTNER, partner)
+    off_up = (off_copy(1, off_ref, M_SAME, plus_same), off_copy(3, off_ref, M_OTHER, plus_other))
+    off_down = (off_copy(2, off_ref, P_SAME, minus_same), off_copy(4, off_ref, P_OTHER, minus_other))
     off_far = off_copy(5, offs.at[far_from], FAR, far_to)
 
     def wait_block(slot, f):
-        send(TO_PLUS, f, spec_ref.at[f], slot, plus_same).wait_recv()
+        send(TO_PLUS, f, spec_ref.at[f], slot, partner).wait_recv()
+
+    def wait_offsets(slot):
+        off_copy(0, off_ref, slot, partner).wait_recv()
 
     row = lax.broadcasted_iota(jnp.int32, (8, lanes), 0)
     part = row & 3
@@ -136,7 +179,9 @@
             block = jnp.concatenate(rows, axis=0)
             aug[slot, g * lanes : (g + 1) * lanes, 0 : 8 * nfreq] = block.T.astype(BF16)
 
-    own_table = tables(off_ref[...].reshape(1, groups, lanes))
+    bins_load.wait()
+    off_load.wait()
+    own_table = tables(offs[OWN : OWN + 1])
     put_aug(OWN, own_table, 0)
     late = row >= 4
     cosine = part < 2
@@ -155,12 +200,27 @@
             wim[f, rows, cols] = jnp.concatenate(
                 [imag if n == f else nothing for n in range(nfreq)], axis=0).astype(BF16)
 
-    pl.semaphore_wait(barrier, 5)
-    for copy in off_sends:
-        copy.start()
-    for f in range(nfreq):
-        for copy in sends(f):
+    greeted = 1 + 2 * has_up.astype(jnp.int32) + 2 * has_down.astype(jnp.int32)
+    pl.semaphore_wait(barrier, greeted)
+
+    @pl.when(has_up)
+    def _():
+        for copy in off_up:
             copy.start()
+        to_plus(0).start()
+
+    @pl.when(has_down)
+    def _():
+        for copy in off_down:
+            copy.start()
+        to_minus(0).start()
+
+    off_partner.start()
+    to_partner(0).start()
+    for f in range(1, nfreq):
+        pl.when(has_up)(lambda f=f: to_plus(f).start())
+        pl.when(has_down)(lambda f=f: to_minus(f).start())
+        to_partner(f).start()
 
     half = lanes // 2
     scale = 1.0 / half
@@ -193,9 +253,22 @@
 
     lax.fori_loop(0, nfreq // 2, own_step, 0)
 
-    for slot in (PARTNER, M_SAME, P_SAME, M_OTHER, P_OTHER):
-        off_copy(0, off_ref, slot, partner).wait_recv()
-    off_far.start()
+    wait_offsets(PARTNER)
+
+    @pl.when(has_down)
+    def _():
+        wait_offsets(M_SAME)
+        wait_offsets(M_OTHER)
+
+    @pl.when(has_up)
+    def _():
+        wait_offsets(P_SAME)
+        wait_offsets(P_OTHER)
+
+    @pl.when(sends_far)
+    def _():
+        off_far.start()
+
     table = tables(offs[PARTNER : P_OTHER + 1])
     for slot in range(PARTNER, P_OTHER + 1):
         put_aug(slot, table, slot - PARTNER)
@@ -211,45 +284,80 @@
 
     lax.fori_loop(0, nfreq // 2, partner_step, 0)
 
-    has_m = jnp.where(chip >= 1, 1.0, 0.0).astype(F32)
-    has_p = jnp.where(chip < nchip - 1, 1.0, 0.0).astype(F32)
-    has_far = jnp.where(core == 1, chip < nchip - 2, chip >= 2)
-    has_far = jnp.where(has_far, 1.0, 0.0).astype(F32)
-
     def pair(m_slot, p_slot, f):
         gm = grads(m_slot, f)
         gp = grads(p_slot, f)
-        acc[f] += has_m * terms(m_slot, f, gm) + has_p * terms(p_slot, f, gp)
+        acc[f] += terms(m_slot, f, gm) + terms(p_slot, f, gp)
 
     def near_step(f, carry):
-        wait_block(M_SAME, f)
-        wait_block(P_SAME, f)
-        for copy in forwards(f):
-            copy.start()
+        @pl.when(f == nfreq - 1)
+        def _():
+            pl.when(has_far)(lambda: wait_offsets(FAR))
+            put_aug(FAR, tables(offs[FAR : FAR + 1]), 0)
+
+        @pl.when(has_down)
+        def _():
+            wait_block(M_SAME, f)
+            forward_m(f).start()
+
+        @pl.when(has_up)
+        def _():
+            wait_block(P_SAME, f)
+            forward_p(f).start()
+
+        @pl.when(sends_far)
+        def _():
+            forward_far(f).start()
+
         pair(M_SAME, P_SAME, f)
-        wait_block(M_OTHER, f)
-        wait_block(P_OTHER, f)
+        pl.when(has_down)(lambda: wait_block(M_OTHER, f))
+        pl.when(has_up)(lambda: wait_block(P_OTHER, f))
         pair(M_OTHER, P_OTHER, f)
         return carry
 
     lax.fori_loop(0, nfreq, near_step, 0)
 
-    off_copy(0, off_ref, FAR, partner).wait_recv()
-    put_aug(FAR, tables(offs[FAR : FAR + 1]), 0)
+    def store(f):
+        return pltpu.make_async_copy(res.at[f], out_ref.at[f], out_sem.at[f])
 
     def far_step(f, carry):
-        wait_block(FAR, f)
-        total = acc[f] + has_far * terms(FAR, f, grads(FAR, f))
-        out_ref[f] = total.T * scale
+        pl.when(has_far)(lambda: wait_block(FAR, f))
+        total = acc[f] + terms(FAR, f, grads(FAR, f))
+        res[f] = total.T * scale
+        store(f).start()
         return carry
 
     lax.fori_loop(0, nfreq, far_step, 0)
 
-    for copy in off_sends + (off_far,):
-        copy.wait_send()
+    off_partner.wait_send()
+
+    @pl.when(has_up)
+    def _():
+        for copy in off_up:
+            copy.wait_send()
+
+    @pl.when(has_down)
+    def _():
+        for copy in off_down:
+            copy.wait_send()
+
+    pl.when(sends_far)(lambda: off_far.wait_send())
     for f in range(nfreq):
-        for copy in sends(f) + forwards(f):
-            copy.wait_send()
+        to_partner(f).wait_send()
+
+        @pl.when(has_up)
+        def _():
+            to_plus(f).wait_send()
+            forward_p(f).wait_send()
+
+        @pl.when(has_down)
+        def _():
+            to_minus(f).wait_send()
+            forward_m(f).wait_send()
+
+        pl.when(sends_far)(lambda: forward_far(f).wait_send())
+    for f in range(nfreq):
+        store(f).wait()
 
 
 def local(ndev, spectra, offsets, bins):
@@ -257,19 +365,24 @@
     lanes = 128
     assert width == lanes and nch % lanes == 0 and nfreq % 2 == 0 and 8 * nfreq <= lanes
     assert (nch * spacing_metres) % period_metres == 0
-    vmem = pl.BlockSpec(memory_space=pltpu.VMEM)
+    hbm = pl.BlockSpec(memory_space=pltpu.HBM)
+    args = (bins, offsets.reshape(nch // lanes, lanes), spectra)
     return pl.pallas_call(
         functools.partial(kernel, nfreq, nch, ndev),
         out_shape=jax.ShapeDtypeStruct((nfreq, nch, width), F32),
-        in_specs=[pl.BlockSpec(memory_space=pltpu.SMEM), vmem, pl.BlockSpec(memory_space=pl.ANY)],
-        out_specs=vmem,
+        in_specs=[hbm, hbm, hbm],
+        out_specs=pl.BlockSpec(memory_space=pl.ANY),
         scratch_shapes=[
             pltpu.VMEM((7, nfreq, nch, width), BF16),
             pltpu.VMEM((7, nch, lanes), BF16),
             pltpu.VMEM((nfreq, 2 * lanes, nch), BF16),
             pltpu.VMEM((nfreq, 2 * lanes, nch), BF16),
             pltpu.VMEM((nfreq, width, nch), F32),
+            pltpu.VMEM((nfreq, nch, width), F32),
             pltpu.VMEM((7, nch // lanes, lanes), jnp.int32),
+            pltpu.SMEM((nfreq,), jnp.int32),
+            pltpu.SemaphoreType.DMA((2,)),
+            pltpu.SemaphoreType.DMA((nfreq,)),
             pltpu.SemaphoreType.DMA((nfreq,)),
             pltpu.SemaphoreType.DMA((6, nfreq)),
             pltpu.SemaphoreType.DMA((7, nfreq)),
@@ -277,8 +390,8 @@
             pltpu.SemaphoreType.DMA((7,)),
         ],
         compiler_params=pltpu.CompilerParams(
-            collective_id=0, has_side_effects=True, vmem_limit_bytes=56 << 20),
-    )(bins, offsets.reshape(nch // lanes, lanes), spectra)
+            collective_id=0, has_side_effects=True, vmem_limit_bytes=24 << 20),
+    )(*(pltpu.with_memory_space_constraint(v, pltpu.HBM) for v in args))
 
 
 def solution(mesh):

time: 36.9 us -> 30 us (0.81)
  the two profiles are of different devices: /device:TPU:0 before, /device:TPU:160 now
where the time goes in v2:
time: 30 us; the launch traced here: 29.6 us
  Pallas kernels  28.6 us (95%)
  local copies, waits for them, and re-layouts  0.97 us (3%)
    pallas_call x1, Pallas kernels, local(): pl.pallas_call(functools.partial(kernel, nfreq, nch, ndev), out_shape=jax...  28.6 us
    unnamed x1, local copies, waits for them, and re-layouts  0.97 us

profile of v2, /device:TPU:160, one launch (start us, length us, event | category | flops | bytes accessed | tf_op | source)
XLA Modules:
  0.0 29.6 jit_solution(272535537716786786)
XLA Ops:
  0.0 28.6 %shard_map.37 = f32[4,512,128]{2,1,0:T(8,128)S(1)} custom-call(s32[4]{0:T(128)} %bins_hbm.1, s32[4,128]{1,0:T(4,128)} %bitcast.1, bf16[4,512,128]{2,1,0:T(8,128)(2,1)} %spec_ref.1), custom_call_target="tpu_custom_call" | custom-call | tf_op jit(solution)/shard_map/pallas_call | solution.py:370
  28.6 1.0 %copy.5 = f32[4,512,128]{2,1,0:T(8,128)} copy(f32[4,512,128]{2,1,0:T(8,128)S(1)} %shard_map.37) | data formatting | bytes 2097152

commit v3 on v2

--- a/solution.py
+++ b/solution.py
@@ -17,7 +17,28 @@
 MESH = pl.DeviceIdType.MESH
 
 OWN, PARTNER, M_SAME, P_SAME, M_OTHER, P_OTHER, FAR = range(7)
-TO_PARTNER, TO_PLUS, TO_MINUS, FWD_M, FWD_P, FWD_FAR = range(6)
+TO_PARTNER, TO_PLUS, TO_MINUS, FWD_M, FWD_P, FWD_FAR, DETOUR = range(7)
+
+PLANE = 16
+DETOURS = 1
+
+EVEN = sum(([(M_SAME, f), (P_SAME, f), (M_OTHER, f), (P_OTHER, f)] for f in range(4)), [])
+EVEN = EVEN + [(FAR, f) for f in range(4)]
+
+
+def lopsided(early, early_other, late, late_other):
+    start = [
+        (early, 0), (early, 1), (early_other, 0), (early_other, 1), (early, 2), (late, 0), (early_other, 2),
+        (late_other, 0), (early, 3), (late, 1), (early_other, 3), (late_other, 1)]
+    return start + [
+        (late, 2), (late_other, 2), (late, 3), (FAR, 0), (late_other, 3), (FAR, 1), (FAR, 2), (FAR, 3)]
+
+
+ORDERS = (EVEN, lopsided(P_SAME, P_OTHER, M_SAME, M_OTHER), lopsided(M_SAME, M_OTHER, P_SAME, P_OTHER))
+
+
+def packed(values, bits):
+    return sum(v << (bits * i) for i, v in enumerate(values))
 
 
 def dot(a, b):
@@ -45,8 +66,8 @@
     return high, v - high
 
 
-def kernel(nfreq, nch, ndev, bins_hbm, off_ref, spec_ref, out_ref, blk, aug, wre, wim, acc, res, offs, bins_ref,
-           in_sem, local_sem, out_sem, send_sem, recv_sem, off_send, off_recv):
+def kernel(nfreq, nch, ndev, bins_hbm, off_ref, spec_ref, out_ref, blk, aug, wre, wim, acc, offs, bins_ref,
+           in_sem, local_sem, send_sem, recv_sem, off_send, off_recv, via, via_off, via_recv):
     lanes = 128
     groups = nch // lanes
     me = lax.axis_index("ch")
@@ -65,6 +86,26 @@
     far_from = jnp.where(upward, M_SAME, P_SAME)
     sends_far = has_up & has_down
     has_far = jnp.where(upward, chip < nchip - 2, chip >= 2)
+    def stepped(place):
+        return lax.rem(place + PLANE, PLANE) == 0
+
+    spared = sends_far & jnp.where(upward, stepped(chip + 1), stepped(chip))
+    detours = jnp.where(upward, stepped(chip + 3) & (chip + 4 < nchip), stepped(chip - 2) & (chip >= 4))
+    relays = jnp.where(upward, stepped(chip - 1) & (chip >= 4), stepped(chip + 2) & (chip + 4 < nchip))
+    four_up, four_down = 2 * jnp.minimum(chip + 4, nchip - 1) + core, 2 * jnp.maximum(chip - 4, 0) + core
+    detour_to = jnp.where(upward, four_up, four_down)
+    detour_from = jnp.where(upward, P_SAME, M_SAME)
+    relay_from = jnp.where(upward, four_down, four_up)
+    relay_to = jnp.where(upward, minus_other, plus_other)
+    late_m = (lax.rem(chip, PLANE) == 0) & has_down
+    late_p = (lax.rem(chip + 1, PLANE) == 0) & has_up
+    edge = late_m | late_p
+
+    def coded(first, field, bits):
+        even, m, p = (packed([unit[field] for unit in order[first::2]], bits) for order in ORDERS)
+        return jnp.where(late_m, m, jnp.where(late_p, p, even))
+
+    codes = [(coded(n, 0, 3), coded(n, 1, 2)) for n in range(2)]
 
     barrier = pltpu.get_barrier_semaphore()
 
@@ -82,6 +123,8 @@
         greet(minus_other)
 
     greet(partner)
+    pl.when(detours)(lambda: greet(detour_to))
+    pl.when(relays)(lambda: greet(relay_from))
 
     def own_load(f):
         return pltpu.make_async_copy(spec_ref.at[f], blk.at[OWN, f], local_sem.at[f])
@@ -129,14 +172,19 @@
     def to_partner(f):
         return send(TO_PARTNER, f, spec_ref.at[f], PARTNER, partner)
 
-    def forward_m(f):
-        return send(FWD_M, f, blk.at[M_SAME, f], M_OTHER, partner)
-
-    def forward_p(f):
-        return send(FWD_P, f, blk.at[P_SAME, f], P_OTHER, partner)
+    def forward(slot, f):
+        return send(slot + FWD_M - M_SAME, f, blk.at[slot, f], slot + M_OTHER - M_SAME, partner)
 
     def forward_far(f):
         return send(FWD_FAR, f, blk.at[far_from, f], FAR, far_to)
+
+    def detour(f):
+        return pltpu.make_async_remote_copy(
+            src_ref=blk.at[detour_from, f], dst_ref=via.at[f], send_sem=send_sem.at[DETOUR, f],
+            recv_sem=via_recv.at[f], device_id=(detour_to,), device_id_type=MESH)
+
+    def relay(f):
+        return send(DETOUR, f, via.at[f], FAR, relay_to)
 
     def off_copy(n, src, slot, to):
         return pltpu.make_async_remote_copy(
@@ -147,6 +195,10 @@
     off_up = (off_copy(1, off_ref, M_SAME, plus_same), off_copy(3, off_ref, M_OTHER, plus_other))
     off_down = (off_copy(2, off_ref, P_SAME, minus_same), off_copy(4, off_ref, P_OTHER, minus_other))
     off_far = off_copy(5, offs.at[far_from], FAR, far_to)
+    off_detour = pltpu.make_async_remote_copy(
+        src_ref=offs.at[detour_from], dst_ref=via_off, send_sem=off_send.at[6],
+        recv_sem=via_recv.at[DETOURS], device_id=(detour_to,), device_id_type=MESH)
+    off_relay = off_copy(6, via_off, FAR, relay_to)
 
     def wait_block(slot, f):
         send(TO_PLUS, f, spec_ref.at[f], slot, partner).wait_recv()
@@ -200,27 +252,31 @@
             wim[f, rows, cols] = jnp.concatenate(
                 [imag if n == f else nothing for n in range(nfreq)], axis=0).astype(BF16)
 
-    greeted = 1 + 2 * has_up.astype(jnp.int32) + 2 * has_down.astype(jnp.int32)
-    pl.semaphore_wait(barrier, greeted)
-
-    @pl.when(has_up)
-    def _():
-        for copy in off_up:
-            copy.start()
-        to_plus(0).start()
-
-    @pl.when(has_down)
-    def _():
-        for copy in off_down:
-            copy.start()
-        to_minus(0).start()
-
-    off_partner.start()
-    to_partner(0).start()
-    for f in range(1, nfreq):
-        pl.when(has_up)(lambda f=f: to_plus(f).start())
-        pl.when(has_down)(lambda f=f: to_minus(f).start())
-        to_partner(f).start()
+    def open_links():
+        greeted = 1 + 2 * has_up.astype(jnp.int32) + 2 * has_down.astype(jnp.int32)
+        greeted += (detours | relays).astype(jnp.int32)
+        pl.semaphore_wait(barrier, greeted)
+
+        @pl.when(has_up)
+        def _():
+            for copy in off_up:
+                copy.start()
+            to_plus(0).start()
+
+        @pl.when(has_down)
+        def _():
+            for copy in off_down:
+                copy.start()
+            to_minus(0).start()
+
+        off_partner.start()
+        to_partner(0).start()
+        for f in range(1, nfreq):
+            pl.when(has_up)(lambda f=f: to_plus(f).start())
+            pl.when(has_down)(lambda f=f: to_minus(f).start())
+            to_partner(f).start()
+
+    pl.when(jnp.logical_not(edge))(open_links)
 
     half = lanes // 2
     scale = 1.0 / half
@@ -252,26 +308,10 @@
         return carry
 
     lax.fori_loop(0, nfreq // 2, own_step, 0)
+    pl.when(edge)(open_links)
 
     wait_offsets(PARTNER)
-
-    @pl.when(has_down)
-    def _():
-        wait_offsets(M_SAME)
-        wait_offsets(M_OTHER)
-
-    @pl.when(has_up)
-    def _():
-        wait_offsets(P_SAME)
-        wait_offsets(P_OTHER)
-
-    @pl.when(sends_far)
-    def _():
-        off_far.start()
-
-    table = tables(offs[PARTNER : P_OTHER + 1])
-    for slot in range(PARTNER, P_OTHER + 1):
-        put_aug(slot, table, slot - PARTNER)
+    put_aug(PARTNER, tables(offs[PARTNER : PARTNER + 1]), 0)
 
     def partner_step(i, carry):
         fs = [2 * i, 2 * i + 1]
@@ -284,110 +324,144 @@
 
     lax.fori_loop(0, nfreq // 2, partner_step, 0)
 
-    def pair(m_slot, p_slot, f):
-        gm = grads(m_slot, f)
-        gp = grads(p_slot, f)
-        acc[f] += terms(m_slot, f, gm) + terms(p_slot, f, gp)
-
-    def near_step(f, carry):
-        @pl.when(f == nfreq - 1)
+    @pl.when(has_down)
+    def _():
+        wait_offsets(M_SAME)
+        wait_offsets(M_OTHER)
+
+    @pl.when(has_up)
+    def _():
+        wait_offsets(P_SAME)
+        wait_offsets(P_OTHER)
+
+    @pl.when(sends_far & jnp.logical_not(spared))
+    def _():
+        off_far.start()
+
+    pl.when(detours)(lambda: off_detour.start())
+
+    table = tables(offs[M_SAME : P_OTHER + 1])
+    for slot in range(M_SAME, P_OTHER + 1):
+        put_aug(slot, table, slot - M_SAME)
+
+    def arrive(slot, f):
+        there = jnp.where(slot == FAR, has_far, jnp.where((slot & 1) == 1, has_up, has_down))
+
+        @pl.when(there)
+        def _():
+            wait_block(slot, f)
+
+        @pl.when(there & (slot <= P_SAME))
+        def _():
+            forward(slot, f).start()
+
+        @pl.when(sends_far & (slot == far_from) & jnp.logical_not(spared & (f < DETOURS)))
+        def _():
+            forward_far(f).start()
+
+        @pl.when((slot == FAR) & (f == 0))
         def _():
             pl.when(has_far)(lambda: wait_offsets(FAR))
             put_aug(FAR, tables(offs[FAR : FAR + 1]), 0)
 
+    def deliver(slot, f):
+        @pl.when(slot == FAR)
+        def _():
+            out_ref[f] = acc[f].T * scale
+
+    def sent():
+        off_partner.wait_send()
+
+        @pl.when(has_up)
+        def _():
+            for copy in off_up:
+                copy.wait_send()
+
         @pl.when(has_down)
         def _():
-            wait_block(M_SAME, f)
-            forward_m(f).start()
-
-        @pl.when(has_up)
-        def _():
-            wait_block(P_SAME, f)
-            forward_p(f).start()
-
-        @pl.when(sends_far)
-        def _():
-            forward_far(f).start()
-
-        pair(M_SAME, P_SAME, f)
-        pl.when(has_down)(lambda: wait_block(M_OTHER, f))
-        pl.when(has_up)(lambda: wait_block(P_OTHER, f))
-        pair(M_OTHER, P_OTHER, f)
+            for copy in off_down:
+                copy.wait_send()
+
+        pl.when(sends_far & jnp.logical_not(spared))(lambda: off_far.wait_send())
+        pl.when(detours)(lambda: off_detour.wait_send())
+        pl.when(relays)(lambda: off_relay.wait_send())
+        for f in range(nfreq):
+            to_partner(f).wait_send()
+            pl.when(has_up)(lambda: to_plus(f).wait_send())
+            pl.when(has_down)(lambda: to_minus(f).wait_send())
+
+    def step(i, carry):
+        (slot0, f0), (slot1, f1) = (((slots >> (3 * i)) & 7, (freqs >> (2 * i)) & 3) for slots, freqs in codes)
+        arrive(slot0, f0)
+        arrive(slot1, f1)
+
+        @pl.when((i == 2) & detours)
+        def _():
+            for n in range(DETOURS):
+                detour(n).start()
+
+        @pl.when(i == len(EVEN) // 2 - 1)
+        def _():
+            sent()
+
+        @pl.when((i == 4) & relays)
+        def _():
+            off_detour.wait_recv()
+            off_relay.start()
+            for n in range(DETOURS):
+                detour(n).wait_recv()
+                relay(n).start()
+
+        g0 = grads(slot0, f0)
+        g1 = grads(slot1, f1)
+        acc[f0] += terms(slot0, f0, g0)
+        acc[f1] += terms(slot1, f1, g1)
+        deliver(slot0, f0)
+        deliver(slot1, f1)
         return carry
 
-    lax.fori_loop(0, nfreq, near_step, 0)
-
-    def store(f):
-        return pltpu.make_async_copy(res.at[f], out_ref.at[f], out_sem.at[f])
-
-    def far_step(f, carry):
-        pl.when(has_far)(lambda: wait_block(FAR, f))
-        total = acc[f] + terms(FAR, f, grads(FAR, f))
-        res[f] = total.T * scale
-        store(f).start()
-        return carry
-
-    lax.fori_loop(0, nfreq, far_step, 0)
-
-    off_partner.wait_send()
-
-    @pl.when(has_up)
-    def _():
-        for copy in off_up:
-            copy.wait_send()
-
-    @pl.when(has_down)
-    def _():
-        for copy in off_down:
-            copy.wait_send()
-
-    pl.when(sends_far)(lambda: off_far.wait_send())
+    lax.fori_loop(0, len(EVEN) // 2, step, 0)
+
     for f in range(nfreq):
-        to_partner(f).wait_send()
-
-        @pl.when(has_up)
-        def _():
-            to_plus(f).wait_send()
-            forward_p(f).wait_send()
-
-        @pl.when(has_down)
-        def _():
-            to_minus(f).wait_send()
-            forward_m(f).wait_send()
-
-        pl.when(sends_far)(lambda: forward_far(f).wait_send())
-    for f in range(nfreq):
-        store(f).wait()
+        pl.when(has_up)(lambda: forward(P_SAME, f).wait_send())
+        pl.when(has_down)(lambda: forward(M_SAME, f).wait_send())
+        if f < DETOURS:
+            pl.when(sends_far & jnp.logical_not(spared))(lambda: forward_far(f).wait_send())
+            pl.when(detours)(lambda: detour(f).wait_send())
+            pl.when(relays)(lambda: relay(f).wait_send())
+        else:
+            pl.when(sends_far)(lambda: forward_far(f).wait_send())
 
 
 def local(ndev, spectra, offsets, bins):
     nfreq, nch, width = spectra.shape
     lanes = 128
     assert width == lanes and nch % lanes == 0 and nfreq % 2 == 0 and 8 * nfreq <= lanes
-    assert (nch * spacing_metres) % period_metres == 0
+    assert (nch * spacing_metres) % period_metres == 0 and nfreq == 4
     hbm = pl.BlockSpec(memory_space=pltpu.HBM)
     args = (bins, offsets.reshape(nch // lanes, lanes), spectra)
     return pl.pallas_call(
         functools.partial(kernel, nfreq, nch, ndev),
         out_shape=jax.ShapeDtypeStruct((nfreq, nch, width), F32),
         in_specs=[hbm, hbm, hbm],
-        out_specs=pl.BlockSpec(memory_space=pl.ANY),
+        out_specs=pl.BlockSpec(memory_space=pltpu.VMEM),
         scratch_shapes=[
             pltpu.VMEM((7, nfreq, nch, width), BF16),
             pltpu.VMEM((7, nch, lanes), BF16),
             pltpu.VMEM((nfreq, 2 * lanes, nch), BF16),
             pltpu.VMEM((nfreq, 2 * lanes, nch), BF16),
             pltpu.VMEM((nfreq, width, nch), F32),
-            pltpu.VMEM((nfreq, nch, width), F32),
             pltpu.VMEM((7, nch // lanes, lanes), jnp.int32),
             pltpu.SMEM((nfreq,), jnp.int32),
             pltpu.SemaphoreType.DMA((2,)),
             pltpu.SemaphoreType.DMA((nfreq,)),
-            pltpu.SemaphoreType.DMA((nfreq,)),
-            pltpu.SemaphoreType.DMA((6, nfreq)),
             pltpu.SemaphoreType.DMA((7, nfreq)),
-            pltpu.SemaphoreType.DMA((6,)),
+            pltpu.SemaphoreType.DMA((7, nfreq)),
             pltpu.SemaphoreType.DMA((7,)),
+            pltpu.SemaphoreType.DMA((7,)),
+            pltpu.VMEM((DETOURS, nch, width), BF16),
+            pltpu.VMEM((nch // lanes, lanes), jnp.int32),
+            pltpu.SemaphoreType.DMA((DETOURS + 1,)),
         ],
         compiler_params=pltpu.CompilerParams(
             collective_id=0, has_side_effects=True, vmem_limit_bytes=24 << 20),

time: 30 us -> 28.6 us (0.953)
  Pallas kernels: 28.6 us -> 27.4 us
    pallas_call x1, Pallas kernels: 28.6 us -> 27.4 us  [local(): pl.pallas_call(functools.partial(kernel, nfreq, nch, ndev), out_shape=jax...]
where the time goes in v3:
time: 28.6 us; the launch traced here: 28.4 us
  Pallas kernels  27.4 us (96%)
  local copies, waits for them, and re-layouts  0.97 us (3%)
    pallas_call x1, Pallas kernels, local(): pl.pallas_call(functools.partial(kernel, nfreq, nch, ndev), out_shape=jax...  27.4 us
    unnamed x1, local copies, waits for them, and re-layouts  0.97 us

profile of v3, /device:TPU:160, one launch (start us, length us, event | category | flops | bytes accessed | tf_op | source)
XLA Modules:
  0.0 28.4 jit_solution(1859315712080565840)
XLA Ops:
  0.0 27.4 %shard_map.37 = f32[4,512,128]{2,1,0:T(8,128)S(1)} custom-call(s32[4]{0:T(128)} %bins_hbm.1, s32[4,128]{1,0:T(4,128)} %bitcast.1, bf16[4,512,128]{2,1,0:T(8,128)(2,1)} %spec_ref.1), custom_call_target="tpu_custom_call" | custom-call | tf_op jit(solution)/shard_map/pallas_call | solution.py:443
  27.4 1.0 %copy.5 = f32[4,512,128]{2,1,0:T(8,128)} copy(f32[4,512,128]{2,1,0:T(8,128)S(1)} %shard_map.37) | data formatting | bytes 2097152

commit v4 on v3

--- a/solution.py
+++ b/solution.py
@@ -19,11 +19,13 @@
 OWN, PARTNER, M_SAME, P_SAME, M_OTHER, P_OTHER, FAR = range(7)
 TO_PARTNER, TO_PLUS, TO_MINUS, FWD_M, FWD_P, FWD_FAR, DETOUR = range(7)
 
-PLANE = 16
+PLANE, ROW = 16, 4
 DETOURS = 1
-
-EVEN = sum(([(M_SAME, f), (P_SAME, f), (M_OTHER, f), (P_OTHER, f)] for f in range(4)), [])
-EVEN = EVEN + [(FAR, f) for f in range(4)]
+ALONE = 4
+
+def even(one, one_other, two, two_other):
+    near = sum(([(one, f), (two, f), (one_other, f), (two_other, f)] for f in range(4)), [])
+    return near + [(FAR, f) for f in range(4)]
 
 
 def lopsided(early, early_other, late, late_other):
@@ -31,10 +33,11 @@
         (early, 0), (early, 1), (early_other, 0), (early_other, 1), (early, 2), (late, 0), (early_other, 2),
         (late_other, 0), (early, 3), (late, 1), (early_other, 3), (late_other, 1)]
     return start + [
-        (late, 2), (late_other, 2), (late, 3), (FAR, 0), (late_other, 3), (FAR, 1), (FAR, 2), (FAR, 3)]
-
-
-ORDERS = (EVEN, lopsided(P_SAME, P_OTHER, M_SAME, M_OTHER), lopsided(M_SAME, M_OTHER, P_SAME, P_OTHER))
+        (late, 2), (FAR, 0), (late_other, 2), (FAR, 1), (late, 3), (FAR, 2), (late_other, 3), (FAR, 3)]
+
+
+M_FIRST, P_FIRST = (M_SAME, M_OTHER, P_SAME, P_OTHER), (P_SAME, P_OTHER, M_SAME, M_OTHER)
+ORDERS = (even(*M_FIRST), even(*P_FIRST), lopsided(*P_FIRST), lopsided(*M_FIRST))
 
 
 def packed(values, bits):
@@ -67,7 +70,7 @@
 
 
 def kernel(nfreq, nch, ndev, bins_hbm, off_ref, spec_ref, out_ref, blk, aug, wre, wim, acc, offs, bins_ref,
-           in_sem, local_sem, send_sem, recv_sem, off_send, off_recv, via, via_off, via_recv):
+           in_sem, local_sem, send_sem, recv_sem, off_send, off_recv, via, via_off, via_recv, token):
     lanes = 128
     groups = nch // lanes
     me = lax.axis_index("ch")
@@ -97,15 +100,29 @@
     detour_from = jnp.where(upward, P_SAME, M_SAME)
     relay_from = jnp.where(upward, four_down, four_up)
     relay_to = jnp.where(upward, minus_other, plus_other)
+    crosses = jnp.where(upward, stepped(chip + 2) & (chip + 3 < nchip), stepped(chip - 1) & (chip >= 3))
+    cross_to = jnp.where(
+        upward, 2 * jnp.minimum(chip + 3, nchip - 1), 2 * jnp.maximum(chip - 3, 0) + 1)
+    crossed = sends_far & jnp.where(upward, stepped(chip), stepped(chip + 1))
+    tells = jnp.where(upward, stepped(chip + 1) & has_up, stepped(chip) & has_down)
+    told = jnp.where(upward, minus_same, plus_same)
     late_m = (lax.rem(chip, PLANE) == 0) & has_down
     late_p = (lax.rem(chip + 1, PLANE) == 0) & has_up
     edge = late_m | late_p
-
-    def coded(first, field, bits):
-        even, m, p = (packed([unit[field] for unit in order[first::2]], bits) for order in ORDERS)
-        return jnp.where(late_m, m, jnp.where(late_p, p, even))
-
-    codes = [(coded(n, 0, 3), coded(n, 1, 2)) for n in range(2)]
+    p_early = lax.rem(chip, ROW) < 2
+
+    def coded(units, field, bits):
+        m_first, p_first, m, p = (packed([unit[field] for unit in order[units]], bits) for order in ORDERS)
+        return jnp.where(late_m, m, jnp.where(late_p, p, jnp.where(p_early, p_first, m_first)))
+
+    units = len(ORDERS[0])
+    codes = [(coded(slice(n, None, 2), 0, 3), coded(slice(n, None, 2), 1, 2)) for n in range(2)]
+    alone = coded(slice(units - ALONE, None), 0, 3), coded(slice(units - ALONE, None), 1, 2)
+    singles = jnp.where(edge, 0, ALONE)
+    pairs = (units - singles) // 2
+
+    def unit_at(code, i):
+        return (code[0] >> (3 * i)) & 7, (code[1] >> (2 * i)) & 3
 
     barrier = pltpu.get_barrier_semaphore()
 
@@ -182,6 +199,9 @@
         return pltpu.make_async_remote_copy(
             src_ref=blk.at[detour_from, f], dst_ref=via.at[f], send_sem=send_sem.at[DETOUR, f],
             recv_sem=via_recv.at[f], device_id=(detour_to,), device_id_type=MESH)
+
+    def cross():
+        return send(DETOUR, nfreq - 1, blk.at[detour_from, nfreq - 1], FAR, cross_to)
 
     def relay(f):
         return send(DETOUR, f, via.at[f], FAR, relay_to)
@@ -259,15 +279,15 @@
 
         @pl.when(has_up)
         def _():
+            to_plus(0).start()
             for copy in off_up:
                 copy.start()
-            to_plus(0).start()
 
         @pl.when(has_down)
         def _():
+            to_minus(0).start()
             for copy in off_down:
                 copy.start()
-            to_minus(0).start()
 
         off_partner.start()
         to_partner(0).start()
@@ -355,7 +375,13 @@
         def _():
             forward(slot, f).start()
 
-        @pl.when(sends_far & (slot == far_from) & jnp.logical_not(spared & (f < DETOURS)))
+        @pl.when(tells & (slot == detour_from) & (f == 0))
+        def _():
+            pl.semaphore_signal(token, inc=1, device_id=(told,), device_id_type=MESH)
+
+        elsewhere = (spared & (f < DETOURS)) | (crossed & (f == nfreq - 1))
+
+        @pl.when(sends_far & (slot == far_from) & jnp.logical_not(elsewhere))
         def _():
             forward_far(f).start()
 
@@ -391,26 +417,28 @@
             pl.when(has_down)(lambda: to_minus(f).wait_send())
 
     def step(i, carry):
-        (slot0, f0), (slot1, f1) = (((slots >> (3 * i)) & 7, (freqs >> (2 * i)) & 3) for slots, freqs in codes)
+        (slot0, f0), (slot1, f1) = (unit_at(code, i) for code in codes)
         arrive(slot0, f0)
         arrive(slot1, f1)
 
-        @pl.when((i == 2) & detours)
-        def _():
-            for n in range(DETOURS):
-                detour(n).start()
-
-        @pl.when(i == len(EVEN) // 2 - 1)
-        def _():
-            sent()
-
-        @pl.when((i == 4) & relays)
+        for n in range(DETOURS):
+            pl.when((i == 2 * n) & detours)(lambda n=n: detour(n).start())
+
+        @pl.when((i == 2) & relays)
         def _():
             off_detour.wait_recv()
             off_relay.start()
-            for n in range(DETOURS):
+
+        for n in range(DETOURS):
+            @pl.when((i == 2 * n + 2) & relays)
+            def _():
                 detour(n).wait_recv()
                 relay(n).start()
+
+        @pl.when((i == 2 * nfreq - 2) & crosses)
+        def _():
+            pl.semaphore_wait(token, 1)
+            cross().start()
 
         g0 = grads(slot0, f0)
         g1 = grads(slot1, f1)
@@ -420,7 +448,17 @@
         deliver(slot1, f1)
         return carry
 
-    lax.fori_loop(0, len(EVEN) // 2, step, 0)
+    lax.fori_loop(0, pairs, step, 0)
+    sent()
+
+    def last_step(i, carry):
+        slot, f = unit_at(alone, i)
+        arrive(slot, f)
+        acc[f] += terms(slot, f, grads(slot, f))
+        deliver(slot, f)
+        return carry
+
+    lax.fori_loop(0, singles, last_step, 0)
 
     for f in range(nfreq):
         pl.when(has_up)(lambda: forward(P_SAME, f).wait_send())
@@ -429,8 +467,11 @@
             pl.when(sends_far & jnp.logical_not(spared))(lambda: forward_far(f).wait_send())
             pl.when(detours)(lambda: detour(f).wait_send())
             pl.when(relays)(lambda: relay(f).wait_send())
+        elif f < nfreq - 1:
+            pl.when(sends_far)(lambda: forward_far(f).wait_send())
         else:
-            pl.when(sends_far)(lambda: forward_far(f).wait_send())
+            pl.when(sends_far & jnp.logical_not(crossed))(lambda: forward_far(f).wait_send())
+            pl.when(crosses)(lambda: cross().wait_send())
 
 
 def local(ndev, spectra, offsets, bins):
@@ -462,6 +503,7 @@
             pltpu.VMEM((DETOURS, nch, width), BF16),
             pltpu.VMEM((nch // lanes, lanes), jnp.int32),
             pltpu.SemaphoreType.DMA((DETOURS + 1,)),
+            pltpu.SemaphoreType.REGULAR,
         ],
         compiler_params=pltpu.CompilerParams(
             collective_id=0, has_side_effects=True, vmem_limit_bytes=24 << 20),

time: 28.6 us -> 28.4 us (level)
  no operation moved by 1% of the time
where the time goes in v4:
time: 28.4 us; the launch traced here: 28.3 us
  Pallas kernels  27.3 us (96%)
  local copies, waits for them, and re-layouts  0.97 us (3%)
    pallas_call x1, Pallas kernels, local(): pl.pallas_call(functools.partial(kernel, nfreq, nch, ndev), out_shape=jax...  27.3 us
    unnamed x1, local copies, waits for them, and re-layouts  0.97 us

profile of v4, /device:TPU:160, one launch (start us, length us, event | category | flops | bytes accessed | tf_op | source)
XLA Modules:
  0.0 28.3 jit_solution(3562294864604183248)
XLA Ops:
  0.0 27.3 %shard_map.37 = f32[4,512,128]{2,1,0:T(8,128)S(1)} custom-call(s32[4]{0:T(128)} %bins_hbm.1, s32[4,128]{1,0:T(4,128)} %bitcast.1, bf16[4,512,128]{2,1,0:T(8,128)(2,1)} %spec_ref.1), custom_call_target="tpu_custom_call" | custom-call | tf_op jit(solution)/shard_map/pallas_call | solution.py:484
  27.3 1.0 %copy.5 = f32[4,512,128]{2,1,0:T(8,128)} copy(f32[4,512,128]{2,1,0:T(8,128)S(1)} %shard_map.37) | data formatting | bytes 2097152

commit v5 on v4

--- a/solution.py
+++ b/solution.py
@@ -20,7 +20,7 @@
 TO_PARTNER, TO_PLUS, TO_MINUS, FWD_M, FWD_P, FWD_FAR, DETOUR = range(7)
 
 PLANE, ROW = 16, 4
-DETOURS = 1
+DETOURS, DETOURS_DOWN = 2, 1
 ALONE = 4
 
 def even(one, one_other, two, two_other):
@@ -33,7 +33,7 @@
         (early, 0), (early, 1), (early_other, 0), (early_other, 1), (early, 2), (late, 0), (early_other, 2),
         (late_other, 0), (early, 3), (late, 1), (early_other, 3), (late_other, 1)]
     return start + [
-        (late, 2), (FAR, 0), (late_other, 2), (FAR, 1), (late, 3), (FAR, 2), (late_other, 3), (FAR, 3)]
+        (late, 2), (FAR, 0), (late_other, 2), (late, 3), (late_other, 3), (FAR, 1), (FAR, 2), (FAR, 3)]
 
 
 M_FIRST, P_FIRST = (M_SAME, M_OTHER, P_SAME, P_OTHER), (P_SAME, P_OTHER, M_SAME, M_OTHER)
@@ -92,6 +92,7 @@
     def stepped(place):
         return lax.rem(place + PLANE, PLANE) == 0
 
+    spared_bins = jnp.where(upward, DETOURS, DETOURS_DOWN)
     spared = sends_far & jnp.where(upward, stepped(chip + 1), stepped(chip))
     detours = jnp.where(upward, stepped(chip + 3) & (chip + 4 < nchip), stepped(chip - 2) & (chip >= 4))
     relays = jnp.where(upward, stepped(chip - 1) & (chip >= 4), stepped(chip + 2) & (chip + 4 < nchip))
@@ -181,13 +182,13 @@
             recv_sem=recv_sem.at[slot, f], device_id=(to,), device_id_type=MESH)
 
     def to_plus(f):
-        return send(TO_PLUS, f, spec_ref.at[f], M_SAME, plus_same)
+        return send(TO_PLUS, f, blk.at[OWN, f], M_SAME, plus_same)
 
     def to_minus(f):
-        return send(TO_MINUS, f, spec_ref.at[f], P_SAME, minus_same)
+        return send(TO_MINUS, f, blk.at[OWN, f], P_SAME, minus_same)
 
     def to_partner(f):
-        return send(TO_PARTNER, f, spec_ref.at[f], PARTNER, partner)
+        return send(TO_PARTNER, f, blk.at[OWN, f], PARTNER, partner)
 
     def forward(slot, f):
         return send(slot + FWD_M - M_SAME, f, blk.at[slot, f], slot + M_OTHER - M_SAME, partner)
@@ -296,6 +297,8 @@
             pl.when(has_down)(lambda f=f: to_minus(f).start())
             to_partner(f).start()
 
+    for f in range(nfreq):
+        own_load(f).wait()
     pl.when(jnp.logical_not(edge))(open_links)
 
     half = lanes // 2
@@ -318,7 +321,6 @@
     def own_step(i, carry):
         fs = [2 * i, 2 * i + 1]
         for f in fs:
-            own_load(f).wait()
             t, swapped = transposed(OWN, f)
             wre[f, :lanes, :] = t * jnp.array(scale, BF16)
             wim[f, :lanes, :] = swapped * jnp.array(-scale, BF16)
@@ -379,7 +381,7 @@
         def _():
             pl.semaphore_signal(token, inc=1, device_id=(told,), device_id_type=MESH)
 
-        elsewhere = (spared & (f < DETOURS)) | (crossed & (f == nfreq - 1))
+        elsewhere = (spared & (f < spared_bins)) | (crossed & (f == nfreq - 1))
 
         @pl.when(sends_far & (slot == far_from) & jnp.logical_not(elsewhere))
         def _():
@@ -422,7 +424,7 @@
         arrive(slot1, f1)
 
         for n in range(DETOURS):
-            pl.when((i == 2 * n) & detours)(lambda n=n: detour(n).start())
+            pl.when((i == 2 * n) & detours & (n < spared_bins))(lambda n=n: detour(n).start())
 
         @pl.when((i == 2) & relays)
         def _():
@@ -430,7 +432,7 @@
             off_relay.start()
 
         for n in range(DETOURS):
-            @pl.when((i == 2 * n + 2) & relays)
+            @pl.when((i == 2 * n + 2) & relays & (n < spared_bins))
             def _():
                 detour(n).wait_recv()
                 relay(n).start()
@@ -464,9 +466,9 @@
         pl.when(has_up)(lambda: forward(P_SAME, f).wait_send())
         pl.when(has_down)(lambda: forward(M_SAME, f).wait_send())
         if f < DETOURS:
-            pl.when(sends_far & jnp.logical_not(spared))(lambda: forward_far(f).wait_send())
-            pl.when(detours)(lambda: detour(f).wait_send())
-            pl.when(relays)(lambda: relay(f).wait_send())
+            pl.when(sends_far & jnp.logical_not(spared & (f < spared_bins)))(lambda: forward_far(f).wait_send())
+            pl.when(detours & (f < spared_bins))(lambda: detour(f).wait_send())
+            pl.when(relays & (f < spared_bins))(lambda: relay(f).wait_send())
         elif f < nfreq - 1:
             pl.when(sends_far)(lambda: forward_far(f).wait_send())
         else:

time: 28.4 us -> 28.1 us (0.989); the launches traced: 28.3 us -> 27.6 us
  Pallas kernels: 27.3 us -> 26.6 us
    pallas_call x1, Pallas kernels: 27.3 us -> 26.6 us  [local(): pl.pallas_call(functools.partial(kernel, nfreq, nch, ndev), out_shape=jax...]
where the time goes in v5:
time: 28.1 us; the launch traced here: 27.6 us
  Pallas kernels  26.6 us (95%)
  local copies, waits for them, and re-layouts  0.97 us (3%)
    pallas_call x1, Pallas kernels, local(): pl.pallas_call(functools.partial(kernel, nfreq, nch, ndev), out_shape=jax...  26.6 us
    unnamed x1, local copies, waits for them, and re-layouts  0.97 us

profile of v5, /device:TPU:160, one launch (start us, length us, event | category | flops | bytes accessed | tf_op | source)
XLA Modules:
  0.0 27.6 jit_solution(16412892968840368802)
XLA Ops:
  0.0 26.6 %shard_map.37 = f32[4,512,128]{2,1,0:T(8,128)S(1)} custom-call(s32[4]{0:T(128)} %bins_hbm.1, s32[4,128]{1,0:T(4,128)} %bitcast.1, bf16[4,512,128]{2,1,0:T(8,128)(2,1)} %spec_ref.1), custom_call_target="tpu_custom_call" | custom-call | tf_op jit(solution)/shard_map/pallas_call | solution.py:486
  26.6 1.0 %copy.5 = f32[4,512,128]{2,1,0:T(8,128)} copy(f32[4,512,128]{2,1,0:T(8,128)S(1)} %shard_map.37) | data formatting | bytes 2097152

commit v6 on v5

--- a/solution.py
+++ b/solution.py
@@ -20,7 +20,7 @@
 TO_PARTNER, TO_PLUS, TO_MINUS, FWD_M, FWD_P, FWD_FAR, DETOUR = range(7)
 
 PLANE, ROW = 16, 4
-DETOURS, DETOURS_DOWN = 2, 1
+DETOURS, DETOURS_DOWN = 1, 1
 ALONE = 4
 
 def even(one, one_other, two, two_other):
@@ -299,7 +299,7 @@
 
     for f in range(nfreq):
         own_load(f).wait()
-    pl.when(jnp.logical_not(edge))(open_links)
+    pl.when(jnp.logical_not(late_m))(open_links)
 
     half = lanes // 2
     scale = 1.0 / half
@@ -330,7 +330,7 @@
         return carry
 
     lax.fori_loop(0, nfreq // 2, own_step, 0)
-    pl.when(edge)(open_links)
+    pl.when(late_m)(open_links)
 
     wait_offsets(PARTNER)
     put_aug(PARTNER, tables(offs[PARTNER : PARTNER + 1]), 0)

time: 28.1 us -> 27.2 us (0.968)
  Pallas kernels: 26.6 us -> 25.8 us
    pallas_call x1, Pallas kernels: 26.6 us -> 25.8 us  [local(): pl.pallas_call(functools.partial(kernel, nfreq, nch, ndev), out_shape=jax...]
where the time goes in v6:
time: 27.2 us; the launch traced here: 26.8 us
  Pallas kernels  25.8 us (95%)
  local copies, waits for them, and re-layouts  0.97 us (4%)
    pallas_call x1, Pallas kernels, local(): pl.pallas_call(functools.partial(kernel, nfreq, nch, ndev), out_shape=jax...  25.8 us
    unnamed x1, local copies, waits for them, and re-layouts  0.97 us

profile of v6, /device:TPU:160, one launch (start us, length us, event | category | flops | bytes accessed | tf_op | source)
XLA Modules:
  0.0 26.8 jit_solution(1219493791062369261)
XLA Ops:
  0.0 25.8 %shard_map.37 = f32[4,512,128]{2,1,0:T(8,128)S(1)} custom-call(s32[4]{0:T(128)} %bins_hbm.1, s32[4,128]{1,0:T(4,128)} %bitcast.1, bf16[4,512,128]{2,1,0:T(8,128)(2,1)} %spec_ref.1), custom_call_target="tpu_custom_call" | custom-call | tf_op jit(solution)/shard_map/pallas_call | solution.py:486
  25.8 1.0 %copy.5 = f32[4,512,128]{2,1,0:T(8,128)} copy(f32[4,512,128]{2,1,0:T(8,128)S(1)} %shard_map.37) | data formatting | bytes 2097152

commit v7 on v6

--- a/solution.py
+++ b/solution.py
@@ -119,7 +119,7 @@
     units = len(ORDERS[0])
     codes = [(coded(slice(n, None, 2), 0, 3), coded(slice(n, None, 2), 1, 2)) for n in range(2)]
     alone = coded(slice(units - ALONE, None), 0, 3), coded(slice(units - ALONE, None), 1, 2)
-    singles = jnp.where(edge, 0, ALONE)
+    singles = jnp.where(edge, ALONE // 2, ALONE)
     pairs = (units - singles) // 2
 
     def unit_at(code, i):
@@ -460,7 +460,7 @@
         deliver(slot, f)
         return carry
 
-    lax.fori_loop(0, singles, last_step, 0)
+    lax.fori_loop(ALONE - singles, ALONE, last_step, 0)
 
     for f in range(nfreq):
         pl.when(has_up)(lambda: forward(P_SAME, f).wait_send())

time: 27.2 us -> 27.1 us (level)
  no operation moved by 1% of the time
where the time goes in v7:
time: 27.1 us; the launch traced here: 26.6 us
  Pallas kernels  25.6 us (94%)
  local copies, waits for them, and re-layouts  0.97 us (4%)
    pallas_call x1, Pallas kernels, local(): pl.pallas_call(functools.partial(kernel, nfreq, nch, ndev), out_shape=jax...  25.6 us
    unnamed x1, local copies, waits for them, and re-layouts  0.97 us

profile of v7, /device:TPU:160, one launch (start us, length us, event | category | flops | bytes accessed | tf_op | source)
XLA Modules:
  0.0 26.6 jit_solution(15349634352772447641)
XLA Ops:
  0.0 25.6 %shard_map.37 = f32[4,512,128]{2,1,0:T(8,128)S(1)} custom-call(s32[4]{0:T(128)} %bins_hbm.1, s32[4,128]{1,0:T(4,128)} %bitcast.1, bf16[4,512,128]{2,1,0:T(8,128)(2,1)} %spec_ref.1), custom_call_target="tpu_custom_call" | custom-call | tf_op jit(solution)/shard_map/pallas_call | solution.py:486
  25.6 1.0 %copy.5 = f32[4,512,128]{2,1,0:T(8,128)} copy(f32[4,512,128]{2,1,0:T(8,128)S(1)} %shard_map.37) | data formatting | bytes 2097152
